TPU v7x, 128 devices: a whole 4x4x4 slice. The times are simulated.
128 devices in a mesh: seq: 32 (over x, y, core), head: 4 (over z).
Axes of the slice: x: 4, y: 4, z: 4, core: 2. Of those that a mesh axis runs over, the one named last changes fastest.
Arguments:
- vis_tokens: bfloat16 [12288, 1408], P('seq'), may hold values from -70 to 70
- vis_counts: int32 [4, 8], replicated, may hold values from 1 to 384, 1536 in all within a row
- vis_spatial: int32 [4, 96], replicated, may hold values from 0 to 1023, as said below
- enc_gain: float32 [1408], replicated, may hold values from 0.25 to 1.75
- enc_bias: float32 [1408], replicated, may hold values from -3 to 3
- enc_qkv: bfloat16 [3, 1408, 1408], P(None, None, 'head'), may hold values from -6 to 6
- enc_proj: bfloat16 [1408, 1408], P('head'), may hold values from -0.15625 to 0.15625
- final_gain: float32 [1408], replicated, may hold values from 0.25 to 1.75
- final_bias: float32 [1408], replicated, may hold values from -3 to 3
- to_decoder: bfloat16 [1408, 512], replicated, may hold values from -0.15625 to 0.15625
- mask_token: float32 [512], replicated, may hold values from -4 to 4
- dec_gain: float32 [512], replicated, may hold values from 0.25 to 1.75
- dec_bias: float32 [512], replicated, may hold values from -3 to 3
- dec_qkv: bfloat16 [3, 512, 512], P(None, None, 'head'), may hold values from -11 to 11
Outputs:
- decoded: bfloat16 [4, 16, 1024, 512], P(None, None, 'seq', 'head')
Inputs may be any that keep to these rules, and one draw needn't show every extreme that they name: `vis_spatial`: row c lists in increasing order the spatial positions visible in every frame of clip c; each aligned run of 32 spatial positions holds exactly 3 of them. The visible tokens of clip c, in order of position, lie on the members of its encoder group in order, vis_counts[c, g] of them on member g; each row sums to 1536.
All inputs are finite; a program needn't handle non-finite values.
Results may differ from a plain program's by a relative error of at most 0.015.
Values may be sent and summed in bfloat16 or wider, within the bound.
A program may use at most 320 MiB of HBM per device.

v0:
```python
import math
import jax
import jax.numpy as jnp
from jax import lax
from jax.sharding import PartitionSpec as P

D = 1408
HEADS = 16
DD = 512
DHEADS = 8
S = 1024
BLOCK = 32
GROUP = 8
L = 16384
VSP = 96
VIS = 1536
epsilon = 1e-06
floor_score = -1e30


def from_partner(block, axis, distance):
    count = lax.axis_size(axis)
    route = []
    for low in range(count):
        high = low | 1 << distance
        if high != low and high < count:
            route += [(low, high), (high, low)]
    return lax.ppermute(block, axis, route)


def layer_norm(values, gain_row, bias_row):
    centre = jnp.mean(values, axis=-1, keepdims=True)
    centred = values - centre
    spread = jnp.mean(centred * centred, axis=-1, keepdims=True)
    return centred * lax.rsqrt(spread + epsilon) * gain_row + bias_row


def sinusoid(positions, table_width):
    column_ids = jnp.arange(table_width, dtype=jnp.int32)
    exponent = (2 * (column_ids // 2)).astype(jnp.float32) / table_width
    frequency = jnp.exp(exponent * -math.log(10000.0))
    angles = positions.astype(jnp.float32)[:, None] * frequency[None, :]
    return jnp.where(column_ids[None, :] % 2 == 0, jnp.sin(angles), jnp.cos(angles))


def fold_block(fold_state, queries, key_rows, value_rows, allowed, score_scale):
    running_max, running_sum, running_acc = fold_state
    scores = jnp.einsum("cqhe,ckhe->chqk", queries, key_rows, preferred_element_type=jnp.float32)
    allowed_grid = allowed[:, None, None, :]
    scores = jnp.where(allowed_grid, scores * score_scale, floor_score)
    new_max = jnp.maximum(running_max, jnp.max(scores, axis=-1))
    factor = jnp.exp(running_max - new_max)
    raised = jnp.where(allowed_grid, jnp.exp(scores - new_max[..., None]), 0.0)
    running_sum = running_sum * factor + jnp.sum(raised, axis=-1)
    weights = raised.astype(jnp.bfloat16)
    update = jnp.einsum("chqk,ckhe->chqe", weights, value_rows, preferred_element_type=jnp.float32)
    running_acc = running_acc * factor[..., None] + update
    return (new_max, running_sum, running_acc)


def empty_state(batch_count, head_count, query_count, head_size):
    return (
        jnp.full((batch_count, head_count, query_count), floor_score, jnp.float32),
        jnp.zeros((batch_count, head_count, query_count), jnp.float32),
        jnp.zeros((batch_count, head_count, query_count, head_size), jnp.float32),
    )


def body(
    vis_tokens,
    vis_counts,
    vis_spatial,
    enc_gain,
    enc_bias,
    enc_qkv,
    enc_proj,
    final_gain,
    final_bias,
    to_decoder,
    mask_token,
    dec_gain,
    dec_bias,
    dec_qkv,
):
    seq_count = lax.axis_size("seq")
    seq_index = lax.axis_index("seq")
    clips = vis_counts.shape[0]
    clip_index = seq_index % clips
    member = seq_index // clips
    slot_count = vis_tokens.shape[0]
    slot_ids = jnp.arange(slot_count, dtype=jnp.int32)
    member_ids = jnp.arange(GROUP, dtype=jnp.int32)
    group_counts = lax.dynamic_index_in_dim(vis_counts, clip_index, 0, keepdims=False)
    before = jnp.sum(jnp.where(member_ids < member, group_counts, 0))
    slot_live = slot_ids < jnp.sum(jnp.where(member_ids == member, group_counts, 0))
    token_rows = vis_tokens.astype(jnp.float32)
    normed = layer_norm(token_rows, enc_gain, enc_bias).astype(jnp.bfloat16)
    enc_parts = [
        jnp.dot(normed, enc_qkv[part_id], preferred_element_type=jnp.float32).astype(jnp.bfloat16)
        for part_id in range(3)
    ]
    head_size = D // HEADS
    enc_width = enc_parts[0].shape[1]
    local_heads = enc_width // head_size
    enc_queries = enc_parts[0].reshape(1, slot_count, local_heads, head_size)
    key_value = jnp.stack([enc_parts[1], enc_parts[2]])
    enc_scale = 1.0 / math.sqrt(head_size)
    clip_bits = clips.bit_length() - 1
    collected = key_value[None]
    for bit in range(GROUP.bit_length() - 1):
        partner = from_partner(collected, "seq", bit + clip_bits)
        upper_side = (member >> bit) % 2 == 1
        collected = jnp.where(
            upper_side,
            jnp.concatenate([partner, collected], axis=0),
            jnp.concatenate([collected, partner], axis=0),
        )
    group_keys = jnp.moveaxis(collected, 1, 0).reshape(
        2, 1, GROUP * slot_count, local_heads, head_size
    )
    group_live = (slot_ids[None, :] < group_counts[:, None]).reshape(1, GROUP * slot_count)
    fold_state = fold_block(
        empty_state(1, local_heads, slot_count, head_size),
        enc_queries,
        group_keys[0],
        group_keys[1],
        group_live,
        enc_scale,
    )
    context = fold_state[2][0] / fold_state[1][0][..., None]
    context = jnp.transpose(context, (1, 0, 2)).reshape(slot_count, enc_width).astype(jnp.bfloat16)
    partial_out = jnp.dot(context, enc_proj, preferred_element_type=jnp.float32)
    attended = lax.psum(partial_out.astype(jnp.bfloat16), "head").astype(jnp.float32)
    residual = token_rows + attended
    final_rows = layer_norm(residual, final_gain, final_bias).astype(jnp.bfloat16)
    encoded = jnp.dot(final_rows, to_decoder, preferred_element_type=jnp.float32).astype(
        jnp.bfloat16
    )
    visible_index = jnp.minimum(before + slot_ids, VIS - 1)
    spatial_row = lax.dynamic_index_in_dim(vis_spatial, clip_index, 0, keepdims=False)
    spatial_ids = jnp.arange(VSP, dtype=jnp.int32)
    spatial = jnp.sum(
        jnp.where((visible_index % VSP)[:, None] == spatial_ids[None, :], spatial_row[None, :], 0),
        axis=1,
    )
    position = visible_index // VSP * S + spatial
    block_index = position // BLOCK
    owner_index = block_index % seq_count
    own_rows = L // seq_count
    local_row = clip_index * own_rows + block_index // seq_count * BLOCK + position % BLOCK
    per_peer = slot_count // seq_count
    peer_ids = jnp.arange(seq_count, dtype=jnp.int32)
    owner_hits = ((owner_index[:, None] == peer_ids[None, :]) & slot_live[:, None]).astype(
        jnp.float32
    )
    earlier_mask = (slot_ids[None, :] < slot_ids[:, None]).astype(jnp.float32)
    earlier = jnp.dot(earlier_mask, owner_hits, precision=lax.Precision.HIGHEST)
    bucket_rank = jnp.sum(earlier * owner_hits, axis=1).astype(jnp.int32)
    target = jnp.where(slot_live, owner_index * per_peer + bucket_rank, -1)
    bucket_ids = jnp.arange(seq_count * per_peer, dtype=jnp.int32)
    chosen = target[None, :] == bucket_ids[:, None]
    send_rows = (
        jnp.dot(chosen.astype(jnp.bfloat16), encoded, preferred_element_type=jnp.float32)
        .astype(jnp.bfloat16)
        .reshape(seq_count, per_peer, DD)
    )
    send_index = jnp.max(jnp.where(chosen, local_row[None, :], -1), axis=1).reshape(
        seq_count, per_peer
    )
    got_rows, got_index = (
        lax.all_to_all(send_rows, "seq", split_axis=0, concat_axis=0, tiled=True),
        lax.all_to_all(send_index, "seq", split_axis=0, concat_axis=0, tiled=True),
    )
    total_rows = clips * own_rows
    got_index = jnp.where(got_index < 0, total_rows, got_index).reshape(-1)
    placed = (
        jnp.zeros((total_rows, DD), jnp.float32)
        .at[got_index]
        .set(got_rows.reshape(-1, DD).astype(jnp.float32), mode="drop")
    )
    row_ids = jnp.arange(own_rows, dtype=jnp.int32)
    local_position = (row_ids // BLOCK * seq_count + seq_index) * BLOCK + row_ids % BLOCK
    frame_ids = jnp.arange(S, dtype=jnp.int32)
    spatial_flags = jnp.any(vis_spatial[:, :, None] == frame_ids[None, None, :], axis=1)
    column_pick = ((local_position % S)[:, None] == frame_ids[None, :]).astype(jnp.float32)
    seen_flags = (
        jnp.einsum(
            "cs,rs->cr",
            spatial_flags.astype(jnp.float32),
            column_pick,
            precision=lax.Precision.HIGHEST,
        )
        > 0.5
    )
    inputs = sinusoid(local_position, DD)[None] + jnp.where(
        seen_flags[..., None], placed.reshape(clips, own_rows, DD), mask_token[None, None, :]
    )
    dec_normed = layer_norm(inputs, dec_gain, dec_bias).astype(jnp.bfloat16)
    dec_size = DD // DHEADS
    dec_query = jnp.einsum(
        "crd,de->cre", dec_normed, dec_qkv[0], preferred_element_type=jnp.float32
    ).astype(jnp.bfloat16)
    dec_width = dec_query.shape[2]
    dec_heads = dec_width // dec_size
    dec_queries = dec_query.reshape(clips, own_rows, dec_heads, dec_size)
    dec_scale = 1.0 / math.sqrt(dec_size)
    start_state = empty_state(clips, dec_heads, own_rows, dec_size)
    dec_key = jnp.einsum(
        "crd,de->cre", dec_normed, dec_qkv[1], preferred_element_type=jnp.float32
    ).astype(jnp.bfloat16)
    dec_value = jnp.einsum(
        "crd,de->cre", dec_normed, dec_qkv[2], preferred_element_type=jnp.float32
    ).astype(jnp.bfloat16)
    stacked = jnp.stack([dec_key, dec_value])
    shard_part = lax.all_gather(stacked, "seq", axis=2, tiled=True)
    row_count = shard_part.shape[2]
    block_count = row_count // own_rows
    block_rows = row_count // block_count
    grouped = jnp.moveaxis(
        shard_part.reshape(2, clips, block_count, block_rows, dec_heads, dec_size), 2, 0
    )
    everywhere = jnp.ones((clips, block_rows), dtype=bool)

    def scan_step(inner_state, key_block):
        return (
            fold_block(inner_state, dec_queries, key_block[0], key_block[1], everywhere, dec_scale),
            None,
        )

    result_state, _ = lax.scan(scan_step, start_state, grouped)
    fold_state = result_state
    dec_context = fold_state[2] / fold_state[1][..., None]
    dec_context = jnp.transpose(dec_context, (0, 2, 1, 3)).reshape(
        clips, own_rows // BLOCK, BLOCK, dec_width
    )
    return dec_context.astype(jnp.bfloat16)


def solution(mesh):
    in_specs = (
        P("seq", None),
        P(),
        P(),
        P(),
        P(),
        P(None, None, "head"),
        P("head", None),
        P(),
        P(),
        P(),
        P(),
        P(),
        P(),
        P(None, None, "head"),
    )
    out_specs = P(None, None, "seq", "head")
    return jax.shard_map(body, mesh=mesh, in_specs=in_specs, out_specs=out_specs, check_vma=False)
```

profile of v0, /device:TPU:1, one launch (start us, length us, event | category | flops | bytes accessed | tf_op | source)
XLA Modules:
  0.0 682.2 jit_solution(31880487049167066)
XLA Ops:
  14.1 3.8 collective-permute-start
  17.9 11.9 %collective-permute-done = bf16[1,2,384,352]{2,3,1,0:T(8,128)(2,1)} collective-permute-done((bf16[1,2,384,352]{2,3,1,0:T(8,128)(2,1)S(1)}, bf16[1,2,384,352]{2,3,1,0:T(8,128)(2,1)}, u32[]{:S(2)}, u32[]{:S(2)}) %collective-permute-start) | collective-permute-done | bytes 540704 | tf_op jit(solution)/shard_map/ppermute | solution.py:28
  33.3 23.1 %collective-permute-done.1 = bf16[2,2,384,352]{2,3,1,0:T(8,128)(2,1)} collective-permute-done((bf16[2,2,384,352]{2,3,1,0:T(8,128)(2,1)}, bf16[2,2,384,352]{2,3,1,0:T(8,128)(2,1)}, u32[]{:S(2)}, u32[]{:S(2)}) %collective-permute-start.1) | collective-permute-done | bytes 1081376 | tf_op jit(solution)/shard_map/ppermute | solution.py:28
  56.4 4.0 maximum_select_fusion.1
  68.0 40.4 %collective-permute-done.2 = bf16[4,2,384,352]{2,3,1,0:T(8,128)(2,1)} collective-permute-done((bf16[4,2,384,352]{2,3,1,0:T(8,128)(2,1)}, bf16[4,2,384,352]{2,3,1,0:T(8,128)(2,1)}, u32[]{:S(2)}, u32[]{:S(2)}) %collective-permute-start.2) | collective-permute-done | bytes 2162720 | tf_op jit(solution)/shard_map/ppermute | solution.py:28
  108.5 3.9 fusion.22
  116.3 4.2 reshape.477
  120.5 3.7 copy.37
  124.2 4.7 reshape.478
  128.9 11.2 %fusion.16 = (f32[4,384]{1,0:T(4,128)S(1)}, f32[4,384,3072]{2,1,0:T(8,128)}) fusion(pred[3072]{0:T(1024)(128)(4,1)S(1)} %lt.153, bf16[384,4,88]{0,2,1:T(8,128)(2,1)S(1)} %bitcast.138, bf16[3072,4,88]{0,2,1:T(8,128)(2,1)} %reshape.477), kind=kOutput, calls=%fused_computation.24 | convolution fusion | flops 844626432 | bytes 21316608 | tf_op jit(solution)/shard_map/cqhe,ckhe->chqk/dot_general | solution.py:48
  140.1 11.2 %fusion.17 = f32[4,384]{1,0:T(4,128)S(1)} fusion(f32[4,384,3072]{2,1,0:T(8,128)} %get-tuple-element.105, f32[4,384]{1,0:T(4,128)S(1)} %get-tuple-element.103, pred[3072]{0:T(1024)(128)(4,1)S(1)} %lt.153), kind=kLoop, calls=%fused_computation.25 | loop fusion | flops 23591424 | bytes 18889728 | tf_op jit(solution)/shard_map/reduce_sum | solution.py:54
  151.4 12.2 %fusion.62 = bf16[384,4,88]{0,2,1:T(8,128)(2,1)} fusion(bf16[3072,4,88]{0,2,1:T(8,128)(2,1)} %reshape.478, f32[4,384,3072]{2,1,0:T(8,128)} %get-tuple-element.105, f32[4,384]{1,0:T(4,128)S(1)} %get-tuple-element.103, pred[3072]{0:T(1024)(128)(4,1)S(1)} %lt.153, f32[384,4]{0,1:T(4,128)S(1)} %bitcast_add_fusion.1, f32[384,4]{0,1:T(4,128)S(1)} %get-tuple-element.102), kind=kOutput, calls=%fused_computation.86 | convolution fusion | flops 854470656 | bytes 21328896 | tf_op jit(solution)/shard_map/chqk,ckhe->chqe/dot_general | solution.py:56
  168.7 10.2 %all-to-all-start = ((s32[32,1,12]{2,1,0:T(1,128)}), s32[32,1,12]{2,1,0:T(1,128)S(1)}, u32[]{:S(2)}, u32[]{:S(2)}) async-start(s32[32,1,12]{2,1,0:T(1,128)} %bitcast.3), calls=%async_computation | async-start | bytes 32768 | tf_op jit(solution)/shard_map/all_to_all | solution.py:172
  179.9 36.2 %all-reduce.2.cloned.1.call-done = bf16[384,1408]{1,0:T(8,128)(2,1)} async-done(((bf16[384,1408]{1,0:T(8,128)(2,1)}), bf16[384,1408]{1,0:T(8,128)(2,1)}) %all-reduce.2.cloned.1.call-update) | async-done | bytes 1081360 | tf_op jit(solution)/shard_map/psum | solution.py:133
  221.6 9.3 %all-to-all-start.1 = ((bf16[32,12,512]{2,1,0:T(8,128)(2,1)}), bf16[32,12,512]{2,1,0:T(8,128)(2,1)S(1)}, u32[]{:S(2)}, u32[]{:S(2)}) async-start(bf16[32,12,512]{2,1,0:T(8,128)(2,1)} %reshape.479), calls=%async_computation.1 | async-start | bytes 1048576 | tf_op jit(solution)/shard_map/all_to_all | solution.py:171
  231.0 3.7 fusion.57
  236.2 6.3 all-to-all-done.1
  242.6 4.0 scatter_custom_fusion
  246.6 3.0 fusion.23
  257.6 108.6 %all-gather.2.cloned.1.call-done = bf16[2,4,16384,128]{3,2,1,0:T(8,128)(2,1)} async-done(((bf16[2,4,512,128]{3,2,1,0:T(8,128)(2,1)}), bf16[2,4,16384,128]{3,2,1,0:T(8,128)(2,1)}) %all-gather.2.cloned.1.call-update) | async-done | bytes 33554448 | tf_op jit(solution)/shard_map/all_gather | solution.py:215
  366.1 44.1 %copy.38 = bf16[2,4,16384,128]{2,3,1,0:T(8,128)(2,1)} copy(bf16[2,4,16384,128]{3,2,1,0:T(8,128)(2,1)} %all-gather.2.cloned.1.call-done) | data formatting | bytes 67108864 | tf_op jit(solution)/shard_map/all_gather | solution.py:215
  410.2 22.7 %copy.45 = bf16[128,8,32,512]{3,2,1,0:T(8,128)(2,1)} copy(bf16[128,8,32,512]{3,1,2,0:T(8,128)(2,1)} %bitcast.132) | data formatting | bytes 67108864
  432.9 22.9 %copy.40 = bf16[32,2,4,512,2,64]{3,5,4,2,1,0:T(8,128)(2,1)} copy(bf16[32,2,4,512,2,64]{3,0,5,4,2,1:T(8,128)(2,1)} %bitcast.133) | data formatting | bytes 67108864
  455.8 217.1 %while.15 = (s32[]{:T(128)}, f32[4,2,512]{2,1,0:T(2,128)S(1)}, f32[4,2,512]{2,1,0:T(2,128)S(1)}, f32[4,2,512,64]{2,3,1,0:T(8,128)S(1)}, bf16[32,2,4,512,2,64]{3,...) while((s32[]{:T(128)}, f32[4,2,512]{2,1,0:T(2,128)S(1)}, ...), condition=%wide.region_19.20_spmd.clone, body=%wide.region_16.19_spmd.clone.sunk | while | flops 554455040 | bytes 29098120 | solution.py:230
  459.7 2.9 fusion.145
  473.2 2.9 fusion.145
  480.0 2.9 fusion.145
  486.8 2.9 fusion.145
  493.6 2.9 fusion.145
  500.4 2.9 fusion.145
  507.2 2.9 fusion.145
  520.7 2.9 fusion.145
  527.5 2.9 fusion.145
  541.1 2.9 fusion.145
  547.9 2.9 fusion.145
  554.7 2.9 fusion.145
  568.2 2.9 fusion.145
  575.0 2.9 fusion.145
  588.6 2.9 fusion.145
  595.4 2.9 fusion.145
  602.2 2.9 fusion.145
  615.7 2.9 fusion.145
  622.5 2.9 fusion.145
  636.1 2.9 fusion.145
  642.9 2.9 fusion.145
  649.7 2.9 fusion.145
  663.2 2.9 fusion.145
  670.0 2.9 fusion.145
  (266 shorter events, 191.8 us)
Async XLA Ops:
  6.5 211.8 %copy-start = (bf16[1408,512]{1,0:T(8,128)(2,1)S(1)}, bf16[1408,512]{1,0:T(8,128)(2,1)}, u32[]{:S(2)}) copy-start(bf16[1408,512]{1,0:T(8,128)(2,1)} %param.25) | copy-start | bytes 4325380
  6.5 3.3 copy-start.4
  6.5 3.3 copy-start.12
  6.5 3.3 copy-start.13
  6.5 209.5 %all-reduce.2.cloned.1.call-start = ((), (), s32[]{:S(2)}) async-start(), calls=%async_computation.2 | async-start | bytes 2162688 | tf_op jit(solution)/shard_map/psum | solution.py:133
  14.1 15.7 %collective-permute-start = (bf16[1,2,384,352]{2,3,1,0:T(8,128)(2,1)S(1)}, bf16[1,2,384,352]{2,3,1,0:T(8,128)(2,1)}, u32[]{:S(2)}, u32[]{:S(2)}) collective-permute-start(bf16[1,2,384,352]{2,3,1,0:T(8,128)(2,1)S(1)} %maximum_bitcast_fusion), channel_id=1, source_target_pairs={{0,16},{16,0},{4,20},{20,4},{8,24},{24,8},{12,28},{28,12},{32,48},... | collective-permute-start | bytes 1622024 | tf_op jit(solution)/shard_map/ppermute | solution.py:28
  32.2 24.3 %collective-permute-start.1 = (bf16[2,2,384,352]{2,3,1,0:T(8,128)(2,1)}, bf16[2,2,384,352]{2,3,1,0:T(8,128)(2,1)}, u32[]{:S(2)}, u32[]{:S(2)}) collective-permute-start(bf16[2,2,384,352]{2,3,1,0:T(8,128)(2,1)} %maximum_select_fusion.2), channel_id=1, source_target_pairs={{0,32},{32,0},{4,36},{36,4},{8,40},{40,8},{12,44},{44,12},{16,48},... | collective-permute-start | bytes 3244040 | tf_op jit(solution)/shard_map/ppermute | solution.py:28
  33.3 31.1 %copy-start.11 = (s32[4,96]{1,0:T(4,128)S(1)}, s32[4,96]{1,0:T(4,128)}, u32[]{:S(2)}) copy-start(s32[4,96]{1,0:T(4,128)} %param.18) | copy-start | bytes 4612
  60.4 48.1 %collective-permute-start.2 = (bf16[4,2,384,352]{2,3,1,0:T(8,128)(2,1)}, bf16[4,2,384,352]{2,3,1,0:T(8,128)(2,1)}, u32[]{:S(2)}, u32[]{:S(2)}) collective-permute-start(bf16[4,2,384,352]{2,3,1,0:T(8,128)(2,1)} %maximum_select_fusion.1), channel_id=1, source_target_pairs={{0,64},{64,0},{4,68},{68,4},{8,72},{72,8},{12,76},{76,12},{16,80},... | collective-permute-start | bytes 6488072 | tf_op jit(solution)/shard_map/ppermute | solution.py:28
  151.4 12.2 %copy-start.6 = (bf16[352,1408]{1,0:T(8,128)(2,1)S(1)}, bf16[352,1408]{1,0:T(8,128)(2,1)}, u32[]{:S(2)}) copy-start(bf16[352,1408]{1,0:T(8,128)(2,1)} %param.22) | copy-start | bytes 2973700
  168.7 52.9 %all-to-all-start = ((s32[32,1,12]{2,1,0:T(1,128)}), s32[32,1,12]{2,1,0:T(1,128)S(1)}, u32[]{:S(2)}, u32[]{:S(2)}) async-start(s32[32,1,12]{2,1,0:T(1,128)} %bitcast.3), calls=%async_computation | async-start | bytes 32768 | tf_op jit(solution)/shard_map/all_to_all | solution.py:172
  179.8 38.5 %copy-start.14 = (f32[1408]{0:T(1024)S(1)}, f32[1408]{0:T(1024)}, u32[]{:S(2)}) copy-start(f32[1408]{0:T(1024)} %param.24) | copy-start | bytes 16900
  179.8 38.5 %copy-start.15 = (f32[1408]{0:T(1024)S(1)}, f32[1408]{0:T(1024)}, u32[]{:S(2)}) copy-start(f32[1408]{0:T(1024)} %param.23) | copy-start | bytes 16900
  216.1 1.7 copy-start.5
  221.6 20.9 %all-to-all-start.1 = ((bf16[32,12,512]{2,1,0:T(8,128)(2,1)}), bf16[32,12,512]{2,1,0:T(8,128)(2,1)S(1)}, u32[]{:S(2)}, u32[]{:S(2)}) async-start(bf16[32,12,512]{2,1,0:T(8,128)(2,1)} %reshape.479), calls=%async_computation.1 | async-start | bytes 1048576 | tf_op jit(solution)/shard_map/all_to_all | solution.py:171
  230.9 135.2 %all-gather.2.cloned.1.call-start = ((), (), s32[]{:S(2)}) async-start(), calls=%async_computation.3 | async-start | bytes 34603008 | tf_op jit(solution)/shard_map/all_gather | solution.py:215
  242.6 4.0 copy-start.8
  246.6 3.4 copy-start.2
  250.0 1.3 copy-start.9
  250.0 1.3 copy-start.10
  251.4 1.2 copy-start.7
  252.6 1.4 copy-start.3
  672.9 2.2 copy-start.1
Sparse Core Ops, SparseCore 0:
  166.5 49.5 all-reduce.1
  255.2 110.8 all-gather.1
where the time goes:
time: 693 us; the launch traced here: 682 us
  waiting for transfers between devices  227 us (33%)
  matrix products  207 us (30%)
  local copies, waits for them, and re-layouts  115 us (17%)
  other arithmetic  90.4 us (13%)
  starting transfers between devices  27.2 us (4%)
  between operations  14.1 us (2%)
    all_gather x1, waiting for transfers between devices, body(): shard_part = lax.all_gather(stacked, 'seq', axis=2, tiled=True)  109 us
    dot_general x33, matrix products, fold_block(): jnp.einsum('chqk,ckhe->chqe', weights, value_rows, preferred_element_type...  105 us
    dot_general x33, matrix products, fold_block(): jnp.einsum('cqhe,ckhe->chqk', queries, key_rows, preferred_element_type=j...  86.7 us
    ppermute x3, waiting for transfers between devices, from_partner(): return lax.ppermute(block, axis, route)  75.4 us
    reduce_sum x33, other arithmetic, fold_block(): running_sum = running_sum * factor + jnp.sum(raised, axis=-1)  56.9 us
    unnamed x35, local copies, waits for them, and re-layouts  46.1 us
    all_gather x1, local copies, waits for them, and re-layouts, body(): shard_part = lax.all_gather(stacked, 'seq', axis=2, tiled=True)  44.1 us
    psum x1, waiting for transfers between devices, body(): lax.psum(partial_out.astype(jnp.bfloat16), 'head').astype(jnp.float32)  36.2 us
  transfers between devices with their start and end apart: 7, of which 6 were waited for; matrix products, arithmetic and copies ran while one was open for 3% of the time, Pallas kernels for 0%

commit v1 on v0

--- a/solution.py
+++ b/solution.py
@@ -16,6 +16,14 @@
 VIS = 1536
 epsilon = 1e-06
 floor_score = -1e30
+
+
+def divide_trees(tile_in):
+    row_out = jnp.stack([tile_in for _ in range(lax.axis_size("seq"))], axis=0)
+    left_arr = jnp.concatenate(
+        lax.all_to_all(row_out, axis_name="seq", split_axis=0, concat_axis=0), axis=2
+    )
+    return left_arr
 
 
 def from_partner(block, axis, distance):
@@ -212,7 +220,7 @@
         "crd,de->cre", dec_normed, dec_qkv[2], preferred_element_type=jnp.float32
     ).astype(jnp.bfloat16)
     stacked = jnp.stack([dec_key, dec_value])
-    shard_part = lax.all_gather(stacked, "seq", axis=2, tiled=True)
+    shard_part = divide_trees(stacked)
     row_count = shard_part.shape[2]
     block_count = row_count // own_rows
     block_rows = row_count // block_count

time: 693 us -> 1060 us (1.53)
  the two profiles are of different devices: /device:TPU:1 before, /device:TPU:12 now
where the time goes in v1:
time: 1060 us; the launch traced here: 1050 us
  waiting for transfers between devices  669 us (63%)
  matrix products  207 us (20%)
  other arithmetic  89.4 us (8%)
  local copies, waits for them, and re-layouts  37.1 us (4%)
  starting transfers between devices  27.3 us (3%)
  between operations  14.1 us (1%)
    all_to_all x1, waiting for transfers between devices, divide_trees(): lax.all_to_all(row_out, axis_name='seq', split_axis=0, concat_axis=0)  547 us
    dot_general x33, matrix products, fold_block(): jnp.einsum('chqk,ckhe->chqe', weights, value_rows, preferred_element_type...  105 us
    dot_general x33, matrix products, fold_block(): jnp.einsum('cqhe,ckhe->chqk', queries, key_rows, preferred_element_type=j...  86.7 us
    ppermute x3, waiting for transfers between devices, from_partner(): return lax.ppermute(block, axis, route)  80.6 us
    reduce_sum x33, other arithmetic, fold_block(): running_sum = running_sum * factor + jnp.sum(raised, axis=-1)  56.9 us
    psum x1, waiting for transfers between devices, body(): lax.psum(partial_out.astype(jnp.bfloat16), 'head').astype(jnp.float32)  38.1 us
  transfers between devices with their start and end apart: 7, of which 6 were waited for; matrix products, arithmetic and copies ran while one was open for 2% of the time, Pallas kernels for 0%

profile of v1, /device:TPU:12, one launch (start us, length us, event | category | flops | bytes accessed | tf_op | source)
XLA Modules:
  0.0 1045.9 jit_solution(2690552517032975872)
XLA Ops:
  16.4 13.3 %collective-permute-done = bf16[1,2,384,352]{2,3,1,0:T(8,128)(2,1)} collective-permute-done((bf16[1,2,384,352]{2,3,1,0:T(8,128)(2,1)S(1)}, bf16[1,2,384,352]{2,3,1,0:T(8,128)(2,1)}, u32[]{:S(2)}, u32[]{:S(2)}) %collective-permute-start) | collective-permute-done | bytes 540704 | tf_op jit(solution)/shard_map/ppermute | solution.py:36
  33.4 23.9 %collective-permute-done.1 = bf16[2,2,384,352]{2,3,1,0:T(8,128)(2,1)} collective-permute-done((bf16[2,2,384,352]{2,3,1,0:T(8,128)(2,1)}, bf16[2,2,384,352]{2,3,1,0:T(8,128)(2,1)}, u32[]{:S(2)}, u32[]{:S(2)}) %collective-permute-start.1) | collective-permute-done | bytes 1081376 | tf_op jit(solution)/shard_map/ppermute | solution.py:36
  57.2 4.0 maximum_select_fusion.1
  66.7 43.4 %collective-permute-done.2 = bf16[4,2,384,352]{2,3,1,0:T(8,128)(2,1)} collective-permute-done((bf16[4,2,384,352]{2,3,1,0:T(8,128)(2,1)}, bf16[4,2,384,352]{2,3,1,0:T(8,128)(2,1)}, u32[]{:S(2)}, u32[]{:S(2)}) %collective-permute-start.2) | collective-permute-done | bytes 2162720 | tf_op jit(solution)/shard_map/ppermute | solution.py:36
  110.1 3.9 fusion.22
  117.9 4.2 reshape.479
  122.2 3.7 copy.35
  125.8 4.7 reshape.480
  130.5 11.2 %fusion.16 = (f32[4,384]{1,0:T(4,128)S(1)}, f32[4,384,3072]{2,1,0:T(8,128)}) fusion(pred[3072]{0:T(1024)(128)(4,1)S(1)} %lt.153, bf16[384,4,88]{0,2,1:T(8,128)(2,1)S(1)} %bitcast.132, bf16[3072,4,88]{0,2,1:T(8,128)(2,1)} %reshape.479), kind=kOutput, calls=%fused_computation.24 | convolution fusion | flops 844626432 | bytes 21316608 | tf_op jit(solution)/shard_map/cqhe,ckhe->chqk/dot_general | solution.py:56
  141.8 11.2 %fusion.17 = f32[4,384]{1,0:T(4,128)S(1)} fusion(f32[4,384,3072]{2,1,0:T(8,128)} %get-tuple-element.87, f32[4,384]{1,0:T(4,128)S(1)} %get-tuple-element.85, pred[3072]{0:T(1024)(128)(4,1)S(1)} %lt.153), kind=kLoop, calls=%fused_computation.25 | loop fusion | flops 23591424 | bytes 18889728 | tf_op jit(solution)/shard_map/reduce_sum | solution.py:62
  153.0 12.2 %fusion.62 = bf16[384,4,88]{0,2,1:T(8,128)(2,1)} fusion(bf16[3072,4,88]{0,2,1:T(8,128)(2,1)} %reshape.480, f32[4,384,3072]{2,1,0:T(8,128)} %get-tuple-element.87, f32[4,384]{1,0:T(4,128)S(1)} %get-tuple-element.85, pred[3072]{0:T(1024)(128)(4,1)S(1)} %lt.153, f32[384,4]{0,1:T(4,128)S(1)} %bitcast_add_fusion.1, f32[384,4]{0,1:T(4,128)S(1)} %get-tuple-element.84), kind=kOutput, calls=%fused_computation.86 | convolution fusion | flops 854470656 | bytes 21328896 | tf_op jit(solution)/shard_map/chqk,ckhe->chqe/dot_general | solution.py:64
  170.3 7.5 all-to-all-start
  178.8 38.1 %all-reduce.2.cloned.1.call-done = bf16[384,1408]{1,0:T(8,128)(2,1)} async-done(((bf16[384,1408]{1,0:T(8,128)(2,1)}), bf16[384,1408]{1,0:T(8,128)(2,1)}) %all-reduce.2.cloned.1.call-update) | async-done | bytes 1081360 | tf_op jit(solution)/shard_map/psum | solution.py:141
  222.4 7.4 all-to-all-start.1
  229.8 3.7 fusion.57
  235.0 3.0 all-to-all-done.1
  238.1 4.0 scatter_custom_fusion
  242.1 3.0 fusion.23
  250.2 11.0 %stack.20 = bf16[32,2,4,512,128]{3,4,2,1,0:T(8,128)(2,1)} broadcast(bf16[2,4,512,128]{2,3,1,0:T(8,128)(2,1)S(1)} %copy.36), dimensions={1,2,3,4} | broadcast | bytes 34603008 | tf_op jit(solution)/shard_map/stack | solution.py:22
  261.2 8.4 all-to-all-start.2
  272.1 547.5 %all-to-all-done.2 = bf16[32,2,4,512,128]{3,4,2,1,0:T(8,128)(2,1)} async-done(((bf16[32,2,4,512,128]{3,4,2,1,0:T(8,128)(2,1)}), bf16[32,2,4,512,128]{3,4,2,1,0:T(8,128)(2,1)}, u32[]{:S(2)}, u32[]{:S(2)}) %all-to-all-start.2) | async-done | bytes 33554464 | tf_op jit(solution)/shard_map/all_to_all | solution.py:24
  819.5 217.1 %while.15 = (s32[]{:T(128)}, f32[4,2,512]{2,1,0:T(2,128)S(1)}, f32[4,2,512]{2,1,0:T(2,128)S(1)}, f32[4,2,512,64]{2,3,1,0:T(8,128)S(1)}, bf16[32,2,4,512,2,64]{3,...) while((s32[]{:T(128)}, f32[4,2,512]{2,1,0:T(2,128)S(1)}, ...), condition=%wide.region_19.20_spmd.clone, body=%wide.region_16.19_spmd.clone.sunk | while | flops 554455040 | bytes 29098120 | solution.py:238
  830.2 2.9 fusion.145
  836.9 2.9 fusion.145
  850.5 2.9 fusion.145
  857.3 2.9 fusion.145
  864.1 2.9 fusion.145
  877.7 2.9 fusion.145
  884.4 2.9 fusion.145
  891.2 2.9 fusion.145
  898.0 2.9 fusion.145
  904.8 2.9 fusion.145
  911.6 2.9 fusion.145
  925.2 2.9 fusion.145
  931.9 2.9 fusion.145
  938.7 2.9 fusion.145
  945.5 2.9 fusion.145
  952.3 2.9 fusion.145
  959.1 2.9 fusion.145
  972.6 2.9 fusion.145
  979.4 2.9 fusion.145
  986.2 2.9 fusion.145
  993.0 2.9 fusion.145
  999.8 2.9 fusion.145
  1006.6 2.9 fusion.145
  1020.1 2.9 fusion.145
  1026.9 2.9 fusion.145
  1033.7 2.9 fusion.145
  (264 shorter events, 185.8 us)
Async XLA Ops:
  6.5 212.6 %copy-start = (bf16[1408,512]{1,0:T(8,128)(2,1)S(1)}, bf16[1408,512]{1,0:T(8,128)(2,1)}, u32[]{:S(2)}) copy-start(bf16[1408,512]{1,0:T(8,128)(2,1)} %param.25) | copy-start | bytes 4325380
  6.5 3.3 copy-start.4
  6.5 3.3 copy-start.12
  6.5 3.3 copy-start.13
  6.5 210.3 %all-reduce.2.cloned.1.call-start = ((), (), s32[]{:S(2)}) async-start(), calls=%async_computation.3 | async-start | bytes 2162688 | tf_op jit(solution)/shard_map/psum | solution.py:141
  14.1 15.7 %collective-permute-start = (bf16[1,2,384,352]{2,3,1,0:T(8,128)(2,1)S(1)}, bf16[1,2,384,352]{2,3,1,0:T(8,128)(2,1)}, u32[]{:S(2)}, u32[]{:S(2)}) collective-permute-start(bf16[1,2,384,352]{2,3,1,0:T(8,128)(2,1)S(1)} %maximum_bitcast_fusion), channel_id=1, source_target_pairs={{0,16},{16,0},{4,20},{20,4},{8,24},{24,8},{12,28},{28,12},{32,48},... | collective-permute-start | bytes 1622024 | tf_op jit(solution)/shard_map/ppermute | solution.py:36
  32.2 25.1 %collective-permute-start.1 = (bf16[2,2,384,352]{2,3,1,0:T(8,128)(2,1)}, bf16[2,2,384,352]{2,3,1,0:T(8,128)(2,1)}, u32[]{:S(2)}, u32[]{:S(2)}) collective-permute-start(bf16[2,2,384,352]{2,3,1,0:T(8,128)(2,1)} %maximum_select_fusion.2), channel_id=1, source_target_pairs={{0,32},{32,0},{4,36},{36,4},{8,40},{40,8},{12,44},{44,12},{16,48},... | collective-permute-start | bytes 3244040 | tf_op jit(solution)/shard_map/ppermute | solution.py:36
  33.4 29.8 %copy-start.11 = (s32[4,96]{1,0:T(4,128)S(1)}, s32[4,96]{1,0:T(4,128)}, u32[]{:S(2)}) copy-start(s32[4,96]{1,0:T(4,128)} %param.18) | copy-start | bytes 4612
  61.2 48.9 %collective-permute-start.2 = (bf16[4,2,384,352]{2,3,1,0:T(8,128)(2,1)}, bf16[4,2,384,352]{2,3,1,0:T(8,128)(2,1)}, u32[]{:S(2)}, u32[]{:S(2)}) collective-permute-start(bf16[4,2,384,352]{2,3,1,0:T(8,128)(2,1)} %maximum_select_fusion.1), channel_id=1, source_target_pairs={{0,64},{64,0},{4,68},{68,4},{8,72},{72,8},{12,76},{76,12},{16,80},... | collective-permute-start | bytes 6488072 | tf_op jit(solution)/shard_map/ppermute | solution.py:36
  153.0 12.2 %copy-start.6 = (bf16[352,1408]{1,0:T(8,128)(2,1)S(1)}, bf16[352,1408]{1,0:T(8,128)(2,1)}, u32[]{:S(2)}) copy-start(bf16[352,1408]{1,0:T(8,128)(2,1)} %param.22) | copy-start | bytes 2973700
  170.3 52.1 %all-to-all-start = ((s32[32,1,12]{2,1,0:T(1,128)}), s32[32,1,12]{2,1,0:T(1,128)S(1)}, u32[]{:S(2)}, u32[]{:S(2)}) async-start(s32[32,1,12]{2,1,0:T(1,128)} %bitcast.3), calls=%async_computation | async-start | bytes 32768 | tf_op jit(solution)/shard_map/all_to_all | solution.py:180
  178.7 40.4 %copy-start.14 = (f32[1408]{0:T(1024)S(1)}, f32[1408]{0:T(1024)}, u32[]{:S(2)}) copy-start(f32[1408]{0:T(1024)} %param.24) | copy-start | bytes 16900
  178.7 40.4 %copy-start.15 = (f32[1408]{0:T(1024)S(1)}, f32[1408]{0:T(1024)}, u32[]{:S(2)}) copy-start(f32[1408]{0:T(1024)} %param.23) | copy-start | bytes 16900
  216.9 1.7 copy-start.5
  222.4 15.6 %all-to-all-start.1 = ((bf16[32,12,512]{2,1,0:T(8,128)(2,1)}), bf16[32,12,512]{2,1,0:T(8,128)(2,1)S(1)}, u32[]{:S(2)}, u32[]{:S(2)}) async-start(bf16[32,12,512]{2,1,0:T(8,128)(2,1)} %reshape.481), calls=%async_computation.1 | async-start | bytes 1048576 | tf_op jit(solution)/shard_map/all_to_all | solution.py:179
  238.1 4.0 copy-start.8
  242.1 3.4 copy-start.2
  245.5 1.3 copy-start.9
  245.5 1.3 copy-start.10
  246.9 1.2 copy-start.7
  248.1 1.4 copy-start.3
  261.2 558.3 %all-to-all-start.2 = ((bf16[32,2,4,512,128]{3,4,2,1,0:T(8,128)(2,1)}), bf16[32,2,4,512,128]{3,4,2,1,0:T(8,128)(2,1)}, u32[]{:S(2)}, u32[]{:S(2)}) async-start(bf16[32,2,4,512,128]{3,4,2,1,0:T(8,128)(2,1)} %stack.20), calls=%async_computation.2 | async-start | bytes 67108864 | tf_op jit(solution)/shard_map/all_to_all | solution.py:24
  1036.6 2.2 copy-start.1
Sparse Core Ops, SparseCore 0:
  168.1 48.7 all-reduce.1
